TPU v7x, 256 devices: a whole 4x4x8 slice. The times are simulated.
256 devices in a mesh: gx: 8 (over y, core), gy: 32 (over z, x).
Axes of the slice: x: 4, y: 4, z: 8, core: 2. Of those that a mesh axis runs over, the one named last changes fastest.
Arguments:
- right_side: float32 [256, 512, 256], P('gx', 'gy'), may hold values from -8 to 8
- coefficient: float32 [256, 512, 256], P('gx', 'gy'), may hold values from 0.1 to 10
Outputs:
- solution_field: float32 [256, 512, 256], P('gx', 'gy')
- residual: float32 [256, 512, 256], P('gx', 'gy')
All inputs are finite; a program needn't handle non-finite values.
Results may differ from a plain program's by a relative error of at most 0.0003.
Values sent between devices are 32-bit elements; how exact they have to be, the bound alone decides.
A program may use at most 128 MiB of HBM per device.

v0:
```python
from functools import partial
import jax
import jax.numpy as jnp
from jax import lax
from jax.sharding import PartitionSpec as P

LEVELS = 5
PRE = 2
POST = 2
BOTTOM = 8
SMOOTH_LO = 0.5
SMOOTH_HI = 2.0
COARSE_LO = 0.05
COARSE_HI = 2.0


def with_halo(value, sides, width):
    for axis, dim in sides:
        size, length = (lax.axis_size(axis), value.shape[dim])
        up = [(i, (i + 1) % size) for i in range(size - 1)]
        down = [(j, i) for i, j in up]
        last = lax.slice_in_dim(value, length - width, length, axis=dim)
        leading = lax.slice_in_dim(value, 0, width, axis=dim)
        before = lax.ppermute(last, axis, up)
        after = lax.ppermute(leading, axis, down)
        value = jnp.concatenate([before, value, after], axis=dim)
    return value


def harmonic(own, other):
    return 2.0 * own * other / (own + other)


def face_weights(conduct, padded):
    lower_x = jnp.where(padded[:-2, 1:-1, :] > 0.0, padded[:-2, 1:-1, :], conduct)
    upper_x = jnp.where(padded[2:, 1:-1, :] > 0.0, padded[2:, 1:-1, :], conduct)
    lower_y = jnp.where(padded[1:-1, :-2, :] > 0.0, padded[1:-1, :-2, :], conduct)
    upper_y = jnp.where(padded[1:-1, 2:, :] > 0.0, padded[1:-1, 2:, :], conduct)
    edged = jnp.pad(conduct, ((0, 0), (0, 0), (1, 1)), mode="edge")
    lower_z = edged[:, :, :-2]
    upper_z = edged[:, :, 2:]
    faces = [
        harmonic(conduct, other) for other in (lower_x, upper_x, lower_y, upper_y, lower_z, upper_z)
    ]
    total = faces[0] + faces[1] + faces[2] + faces[3] + faces[4] + faces[5]
    return tuple(faces) + (total,)


def stencil(field, padded, weights, scale):
    zpad = jnp.pad(field, ((0, 0), (0, 0), (1, 1)))
    beside = weights[0] * padded[:-2, 1:-1, :] + weights[1] * padded[2:, 1:-1, :]
    beside = beside + weights[2] * padded[1:-1, :-2, :] + weights[3] * padded[1:-1, 2:, :]
    beside = beside + weights[4] * zpad[:, :, :-2] + weights[5] * zpad[:, :, 2:]
    return scale * (weights[6] * field - beside)


def pad_plane(field):
    return jnp.pad(field, ((1, 1), (1, 1), (0, 0)))


def whole_operate(field, weights, scale):
    return stencil(field, pad_plane(field), weights, scale)


def local_operate(field, weights, scale):
    padded = with_halo(field, (("gx", 0), ("gy", 1)), 1)
    return stencil(field, padded, weights, scale)


def chebyshev(source, start, sweeps, low_end, high_end, operate, inverse):
    theta_val = (high_end + low_end) / 2.0
    half_width = (high_end - low_end) / 2.0
    sigma_val = theta_val / half_width
    rho_now = 1.0 / sigma_val
    if start is None:
        update = inverse * source / theta_val
        iterate = update
    else:
        update = inverse * (source - operate(start)) / theta_val
        iterate = start + update
    for sweep_index in range(sweeps - 1):
        rho_next = 1.0 / (2.0 * sigma_val - rho_now)
        update = rho_next * rho_now * update + 2.0 * rho_next / half_width * inverse * (
            source - operate(iterate)
        )
        iterate = iterate + update
        rho_now = rho_next
    return iterate


def restrict(field):
    size_x, size_y, size_z = field.shape
    return jnp.mean(field.reshape(size_x // 2, 2, size_y // 2, 2, size_z // 2, 2), axis=(1, 3, 5))


def prolong(field):
    size_x, size_y, size_z = field.shape
    grown = jnp.broadcast_to(field[:, None, :, None, :, None], (size_x, 2, size_y, 2, size_z, 2))
    return grown.reshape(2 * size_x, 2 * size_y, 2 * size_z)


def cycle(level_index, source, conduct):
    weights = face_weights(conduct, pad_plane(conduct))
    scale = 0.25**level_index
    inverse = 1.0 / (scale * weights[6])
    operate = partial(whole_operate, weights=weights, scale=scale)
    return chebyshev(source, None, BOTTOM, COARSE_LO, COARSE_HI, operate, inverse)


def collect(source, conduct):
    block_x, block_y, block_z = source.shape
    count_x = lax.axis_size("gx")
    count_y = lax.axis_size("gy")
    gathered = (
        lax.all_gather(source, ("gx", "gy"), axis=0, tiled=True),
        lax.all_gather(conduct, ("gx", "gy"), axis=0, tiled=True),
    )
    arranged = []
    for member in gathered:
        blocks = member.reshape(count_x, count_y, block_x, block_y, block_z)
        arranged.append(
            blocks.transpose(0, 2, 1, 3, 4).reshape(count_x * block_x, count_y * block_y, block_z)
        )
    return (arranged[0], arranged[1])


def own_block(whole, shape):
    start_x = lax.axis_index("gx") * shape[0]
    start_y = lax.axis_index("gy") * shape[1]
    return lax.dynamic_slice(whole, (start_x, start_y, jnp.zeros((), jnp.int32)), shape)


def per_device(right_side, coefficient):
    joined = LEVELS - 1
    conducts = [coefficient]
    for level_index in range(1, joined + 1):
        conducts.append(restrict(conducts[-1]))
    operators = []
    inverses = []
    for level_index in range(joined):
        padded = with_halo(conducts[level_index], (("gx", 0), ("gy", 1)), 1)
        weights = face_weights(conducts[level_index], padded)
        scale = 0.25**level_index
        inverses.append(1.0 / (scale * weights[6]))
        operators.append(partial(local_operate, weights=weights, scale=scale))
    sources = [right_side]
    smoothed = []
    for level_index in range(joined):
        operate = operators[level_index]
        iterate = chebyshev(
            sources[level_index], None, PRE, SMOOTH_LO, SMOOTH_HI, operate, inverses[level_index]
        )
        smoothed.append(iterate)
        sources.append(restrict(sources[level_index] - operate(iterate)))
    whole_source, whole_conduct = collect(sources[joined], conducts[joined])
    correction = own_block(cycle(joined, whole_source, whole_conduct), sources[joined].shape)
    for level_index in reversed(range(joined)):
        iterate = smoothed[level_index] + prolong(correction)
        correction = chebyshev(
            sources[level_index],
            iterate,
            POST,
            SMOOTH_LO,
            SMOOTH_HI,
            operators[level_index],
            inverses[level_index],
        )
    residual = right_side - operators[0](correction)
    return (correction, residual)


def solution(mesh):
    in_specs = (P("gx", "gy", None), P("gx", "gy", None))
    out_specs = (P("gx", "gy", None), P("gx", "gy", None))
    return jax.shard_map(
        per_device, mesh=mesh, in_specs=in_specs, out_specs=out_specs, check_vma=False
    )
```

profile of v0, /device:TPU:103, one launch (start us, length us, event | category | flops | bytes accessed | tf_op | source)
XLA Modules:
  0.0 702.0 jit_solution(18021534122502074643)
XLA Ops:
  1.4 3.8 collective-permute-start
  7.2 35.6 %reshape.80 = f32[16,2,8,2,128,2]{5,4,3,2,1,0:T(8,128)} reshape(f32[32,16,256]{2,1,0:T(8,128)} %param.3) | data formatting | bytes 1048576 | tf_op jit(solution)/shard_map/reshape | solution.py:93
  42.8 12.2 %reduce_sum.86 = f32[16,8,128]{2,1,0:T(8,128)S(1)} reduce(f32[16,2,8,2,128,2]{5,4,3,2,1,0:T(8,128)} %reshape.80, f32[]{:T(128)} %constant.35.clone.1), dimensions={1,3,5}, to_apply=%region_0.0 | reduce | flops 114688 | bytes 589828 | tf_op jit(solution)/shard_map/reduce_sum | solution.py:93
  55.6 3.6 collective-permute-start.8
  62.0 5.5 div.203
  70.2 4.7 collective-permute-start.2
  76.9 6.0 collective-permute-done.3
  84.8 5.1 collective-permute-start.4
  92.4 3.6 collective-permute-start.20
  98.1 3.4 collective-permute-start.7
  106.3 3.8 fusion.7
  124.2 6.5 collective-permute-start.10
  134.1 35.6 %reshape.81 = f32[16,2,8,2,128,2]{5,4,3,2,1,0:T(8,128)} reshape(f32[32,16,256]{2,1,0:T(8,128)} %fusion.13) | data formatting | bytes 1048576 | tf_op jit(solution)/shard_map/reshape | solution.py:93
  169.7 12.2 %reduce_sum.87 = f32[16,8,128]{2,1,0:T(8,128)S(1)} reduce(f32[16,2,8,2,128,2]{5,4,3,2,1,0:T(8,128)} %reshape.81, f32[]{:T(128)} %constant.35.clone.1), dimensions={1,3,5}, to_apply=%region_1.0 | reduce | flops 114688 | bytes 589828 | tf_op jit(solution)/shard_map/reduce_sum | solution.py:93
  183.7 4.5 collective-permute-start.16
  191.5 3.6 collective-permute-start.32
  195.1 7.0 collective-permute-start.18
  205.5 4.7 collective-permute-done.19
  229.5 5.3 collective-permute-start.22
  238.6 6.3 reshape.82
  249.2 4.5 collective-permute-start.28
  258.6 7.0 collective-permute-start.30
  267.5 59.7 %all-gather.2 = f32[256,2,16]{2,1,0:T(2,128)S(1)} all-gather(f32[1,2,16]{2,1,0:T(2,128)S(1)} %multiply_bitcast_fusion.1), channel_id=2, replica_groups=mesh['gx'=8,'gy'=32] {'gx','gy'}, dimensions={0}, use_global_device_ids=true | all-gather | bytes 32896 | tf_op jit(solution)/shard_map/all_gather | solution.py:116
  328.2 4.6 collective-permute-start.36
  343.7 6.0 collective-permute-start.34
  358.8 3.9 collective-permute-start.40
  367.6 5.1 collective-permute-start.42
  374.7 3.8 multiply_divide_fusion
  381.7 3.4 collective-permute-start.44
  391.5 3.9 collective-permute-start.46
  397.4 6.0 collective-permute-done.47
  408.4 57.4 %all-gather.3 = f32[256,2,16]{2,1,0:T(2,128)S(1)} all-gather(f32[1,2,16]{2,1,0:T(2,128)S(1)} %multiply_bitcast_fusion), channel_id=3, replica_groups=mesh['gx'=8,'gy'=32] {'gx','gy'}, dimensions={0}, use_global_device_ids=true | all-gather | bytes 32896 | tf_op jit(solution)/shard_map/all_gather | solution.py:115
  479.7 4.6 collective-permute-start.48
  489.3 5.3 collective-permute-start.50
  496.5 5.8 collective-permute-done.51
  513.2 3.4 collective-permute-start.55
  516.6 4.3 collective-permute-done.55
  538.0 4.3 collective-permute-done.59
  556.5 4.3 collective-permute-done.63
  564.4 4.0 reshape.89
  582.6 4.6 collective-permute-done.67
  601.6 4.3 collective-permute-done.71
  607.1 11.4 %broadcast_in_dim.36 = f32[16,2,8,2,128,2]{5,4,3,2,1,0:T(8,128)} broadcast(f32[16,8,128]{2,1,0:T(8,128)S(1)} %fusion.220), dimensions={0,2,4} | broadcast | bytes 589824 | tf_op jit(solution)/shard_map/broadcast_in_dim | solution.py:98
  618.5 24.6 %reshape.90 = f32[32,16,256]{2,1,0:T(8,128)} reshape(f32[16,2,8,2,128,2]{5,4,3,2,1,0:T(8,128)} %broadcast_in_dim.36) | data formatting | bytes 1048576 | tf_op jit(solution)/shard_map/reshape | solution.py:99
  654.5 3.4 collective-permute-start.75
  657.9 4.6 collective-permute-done.75
  676.9 4.6 collective-permute-done.79
  695.9 4.6 collective-permute-done.83
  (313 shorter events, 263.2 us)
Async XLA Ops:
  1.4 68.7 %collective-permute-start = (f32[1,16,256]{2,1,0:T(8,128)S(1)}, f32[1,16,256]{2,1,0:T(8,128)S(1)}, u32[]{:S(2)}, u32[]{:S(2)}) collective-permute-start(f32[1,16,256]{2,1,0:T(8,128)S(1)} %get-tuple-element.81), channel_id=1, source_target_pairs={{0,32},{32,64},{64,96},{96,128},{128,160},{160,192},{192,224},{1,3... | collective-permute-start | bytes 49160 | tf_op jit(solution)/shard_map/ppermute | solution.py:24
  5.2 65.0 %collective-permute-start.1 = (f32[1,16,256]{2,1,0:T(8,128)S(1)}, f32[1,16,256]{2,1,0:T(8,128)S(1)}, u32[]{:S(2)}, u32[]{:S(2)}) collective-permute-start(f32[1,16,256]{2,1,0:T(8,128)S(1)} %get-tuple-element.80), channel_id=1, source_target_pairs={{32,0},{64,32},{96,64},{128,96},{160,128},{192,160},{224,192},{33,... | collective-permute-start | bytes 49160 | tf_op jit(solution)/shard_map/ppermute | solution.py:25
  55.6 65.6 %collective-permute-start.8 = (f32[1,8,128]{2,1,0:T(8,128)}, f32[1,8,128]{2,1,0:T(8,128)}, u32[]{:S(2)}, u32[]{:S(2)}) collective-permute-start(f32[1,8,128]{2,1,0:T(8,128)} %get-tuple-element.104), channel_id=1, source_target_pairs={{0,32},{32,64},{64,96},{96,128},{128,160},{160,192},{192,224},{1,3... | collective-permute-start | bytes 12296 | tf_op jit(solution)/shard_map/ppermute | solution.py:24
  59.3 64.1 %collective-permute-start.9 = (f32[1,8,128]{2,1,0:T(8,128)}, f32[1,8,128]{2,1,0:T(8,128)}, u32[]{:S(2)}, u32[]{:S(2)}) collective-permute-start(f32[1,8,128]{2,1,0:T(8,128)} %get-tuple-element.105), channel_id=1, source_target_pairs={{32,0},{64,32},{96,64},{128,96},{160,128},{192,160},{224,192},{33,... | collective-permute-start | bytes 12296 | tf_op jit(solution)/shard_map/ppermute | solution.py:25
  74.9 8.0 %collective-permute-start.3 = (f32[34,1,256]{2,1,0:T(1,128)S(1)}, f32[34,1,256]{2,1,0:T(1,128)S(1)}, u32[]{:S(2)}, u32[]{:S(2)}) collective-permute-start(f32[34,1,256]{2,1,0:T(1,128)S(1)} %get-tuple-element.66), channel_id=1, source_target_pairs={{1,0},{2,1},{3,2},{4,3},{5,4},{6,5},{7,6},{8,7},{9,8},{10,9},{11,1... | collective-permute-start | bytes 104456 | tf_op jit(solution)/shard_map/ppermute | solution.py:25
  84.8 11.2 %collective-permute-start.4 = (f32[1,16,256]{2,1,0:T(8,128)S(1)}, f32[1,16,256]{2,1,0:T(8,128)S(1)}, u32[]{:S(2)}, u32[]{:S(2)}) collective-permute-start(f32[1,16,256]{2,1,0:T(8,128)S(1)} %get-tuple-element.76), channel_id=1, source_target_pairs={{0,32},{32,64},{64,96},{96,128},{128,160},{160,192},{192,224},{1,3... | collective-permute-start | bytes 49160 | tf_op jit(solution)/shard_map/ppermute | solution.py:24
  92.4 132.4 %collective-permute-start.20 = (f32[1,4,64]{2,1,0:T(4,128)}, f32[1,4,64]{2,1,0:T(4,128)}, u32[]{:S(2)}, u32[]{:S(2)}) collective-permute-start(f32[1,4,64]{2,1,0:T(4,128)} %get-tuple-element.126), channel_id=1, source_target_pairs={{0,32},{32,64},{64,96},{96,128},{128,160},{160,192},{192,224},{1,3... | collective-permute-start | bytes 3080 | tf_op jit(solution)/shard_map/ppermute | solution.py:24
  96.1 8.5 %collective-permute-start.6 = (f32[34,1,256]{2,1,0:T(1,128)S(1)}, f32[34,1,256]{2,1,0:T(1,128)S(1)}, u32[]{:S(2)}, u32[]{:S(2)}) collective-permute-start(f32[34,1,256]{2,1,0:T(1,128)S(1)} %get-tuple-element.64), channel_id=1, source_target_pairs={{0,1},{1,2},{2,3},{3,4},{4,5},{5,6},{6,7},{7,8},{8,9},{9,10},{10,1... | collective-permute-start | bytes 104456 | tf_op jit(solution)/shard_map/ppermute | solution.py:24
  98.1 8.3 %collective-permute-start.7 = (f32[34,1,256]{2,1,0:T(1,128)S(1)}, f32[34,1,256]{2,1,0:T(1,128)S(1)}, u32[]{:S(2)}, u32[]{:S(2)}) collective-permute-start(f32[34,1,256]{2,1,0:T(1,128)S(1)} %get-tuple-element.65), channel_id=1, source_target_pairs={{1,0},{2,1},{3,2},{4,3},{5,4},{6,5},{7,6},{8,7},{9,8},{10,9},{11,1... | collective-permute-start | bytes 104456 | tf_op jit(solution)/shard_map/ppermute | solution.py:25
  116.0 112.1 %collective-permute-start.21 = (f32[1,4,64]{2,1,0:T(4,128)}, f32[1,4,64]{2,1,0:T(4,128)}, u32[]{:S(2)}, u32[]{:S(2)}) collective-permute-start(f32[1,4,64]{2,1,0:T(4,128)} %get-tuple-element.127), channel_id=1, source_target_pairs={{32,0},{64,32},{96,64},{128,96},{160,128},{192,160},{224,192},{33,... | collective-permute-start | bytes 3080 | tf_op jit(solution)/shard_map/ppermute | solution.py:25
  118.1 12.6 %collective-permute-start.14 = (f32[34,1,256]{2,1,0:T(1,128)S(1)}, f32[34,1,256]{2,1,0:T(1,128)S(1)}, u32[]{:S(2)}, u32[]{:S(2)}) collective-permute-start(f32[34,1,256]{2,1,0:T(1,128)S(1)} %get-tuple-element.62), channel_id=1, source_target_pairs={{0,1},{1,2},{2,3},{3,4},{4,5},{5,6},{6,7},{7,8},{8,9},{9,10},{10,1... | collective-permute-start | bytes 104456 | tf_op jit(solution)/shard_map/ppermute | solution.py:24
  121.2 11.3 %collective-permute-start.15 = (f32[34,1,256]{2,1,0:T(1,128)S(1)}, f32[34,1,256]{2,1,0:T(1,128)S(1)}, u32[]{:S(2)}, u32[]{:S(2)}) collective-permute-start(f32[34,1,256]{2,1,0:T(1,128)S(1)} %get-tuple-element.63), channel_id=1, source_target_pairs={{1,0},{2,1},{3,2},{4,3},{5,4},{6,5},{7,6},{8,7},{9,8},{10,9},{11,1... | collective-permute-start | bytes 104456 | tf_op jit(solution)/shard_map/ppermute | solution.py:25
  124.2 57.8 %collective-permute-start.10 = (f32[18,1,128]{2,1,0:T(1,128)S(1)}, f32[18,1,128]{2,1,0:T(1,128)}, u32[]{:S(2)}, u32[]{:S(2)}) collective-permute-start(f32[18,1,128]{2,1,0:T(1,128)S(1)} %get-tuple-element.93), channel_id=1, source_target_pairs={{0,1},{1,2},{2,3},{3,4},{4,5},{5,6},{6,7},{7,8},{8,9},{9,10},{10,1... | collective-permute-start | bytes 27656 | tf_op jit(solution)/shard_map/ppermute | solution.py:24
  130.7 51.3 %collective-permute-start.11 = (f32[18,1,128]{2,1,0:T(1,128)S(1)}, f32[18,1,128]{2,1,0:T(1,128)S(1)}, u32[]{:S(2)}, u32[]{:S(2)}) collective-permute-start(f32[18,1,128]{2,1,0:T(1,128)S(1)} %get-tuple-element.92), channel_id=1, source_target_pairs={{1,0},{2,1},{3,2},{4,3},{5,4},{6,5},{7,6},{8,7},{9,8},{10,9},{11,1... | collective-permute-start | bytes 27656 | tf_op jit(solution)/shard_map/ppermute | solution.py:25
  183.7 11.4 %collective-permute-start.16 = (f32[1,8,128]{2,1,0:T(8,128)S(1)}, f32[1,8,128]{2,1,0:T(8,128)S(1)}, u32[]{:S(2)}, u32[]{:S(2)}) collective-permute-start(f32[1,8,128]{2,1,0:T(8,128)S(1)} %get-tuple-element.100), channel_id=1, source_target_pairs={{0,32},{32,64},{64,96},{96,128},{128,160},{160,192},{192,224},{1,3... | collective-permute-start | bytes 12296 | tf_op jit(solution)/shard_map/ppermute | solution.py:24
  188.2 6.9 collective-permute-start.17
  191.5 144.2 %collective-permute-start.32 = (f32[1,2,32]{2,0,1:T(1,128)}, f32[1,2,32]{2,0,1:T(1,128)}, u32[]{:S(2)}, u32[]{:S(2)}) collective-permute-start(f32[1,2,32]{2,0,1:T(1,128)} %get-tuple-element.150), channel_id=1, source_target_pairs={{0,32},{32,64},{64,96},{96,128},{128,160},{160,192},{192,224},{1,3... | collective-permute-start | bytes 776 | tf_op jit(solution)/shard_map/ppermute | solution.py:24
  195.1 10.4 %collective-permute-start.18 = (f32[18,1,128]{2,1,0:T(1,128)S(1)}, f32[18,1,128]{2,1,0:T(1,128)S(1)}, u32[]{:S(2)}, u32[]{:S(2)}) collective-permute-start(f32[18,1,128]{2,1,0:T(1,128)S(1)} %get-tuple-element.90), channel_id=1, source_target_pairs={{0,1},{1,2},{2,3},{3,4},{4,5},{5,6},{6,7},{7,8},{8,9},{9,10},{10,1... | collective-permute-start | bytes 27656 | tf_op jit(solution)/shard_map/ppermute | solution.py:24
  202.1 8.1 %collective-permute-start.19 = (f32[18,1,128]{2,1,0:T(1,128)S(1)}, f32[18,1,128]{2,1,0:T(1,128)S(1)}, u32[]{:S(2)}, u32[]{:S(2)}) collective-permute-start(f32[18,1,128]{2,1,0:T(1,128)S(1)} %get-tuple-element.91), channel_id=1, source_target_pairs={{1,0},{2,1},{3,2},{4,3},{5,4},{6,5},{7,6},{8,7},{9,8},{10,9},{11,1... | collective-permute-start | bytes 27656 | tf_op jit(solution)/shard_map/ppermute | solution.py:25
  211.0 9.1 %collective-permute-start.24 = (f32[1,8,128]{2,1,0:T(8,128)}, f32[1,8,128]{2,1,0:T(8,128)}, u32[]{:S(2)}, u32[]{:S(2)}) collective-permute-start(f32[1,8,128]{2,1,0:T(8,128)} %get-tuple-element.98), channel_id=1, source_target_pairs={{0,32},{32,64},{64,96},{96,128},{128,160},{160,192},{192,224},{1,3... | collective-permute-start | bytes 12296 | tf_op jit(solution)/shard_map/ppermute | solution.py:24
  214.0 8.1 %collective-permute-start.25 = (f32[1,8,128]{2,1,0:T(8,128)}, f32[1,8,128]{2,1,0:T(8,128)}, u32[]{:S(2)}, u32[]{:S(2)}) collective-permute-start(f32[1,8,128]{2,1,0:T(8,128)} %get-tuple-element.99), channel_id=1, source_target_pairs={{32,0},{64,32},{96,64},{128,96},{160,128},{192,160},{224,192},{33,... | collective-permute-start | bytes 12296 | tf_op jit(solution)/shard_map/ppermute | solution.py:25
  220.1 115.6 %collective-permute-start.33 = (f32[1,2,32]{2,0,1:T(1,128)}, f32[1,2,32]{2,0,1:T(1,128)}, u32[]{:S(2)}, u32[]{:S(2)}) collective-permute-start(f32[1,2,32]{2,0,1:T(1,128)} %get-tuple-element.151), channel_id=1, source_target_pairs={{32,0},{64,32},{96,64},{128,96},{160,128},{192,160},{224,192},{33,... | collective-permute-start | bytes 776 | tf_op jit(solution)/shard_map/ppermute | solution.py:25
  222.8 12.0 %collective-permute-start.26 = (f32[18,1,128]{2,1,0:T(1,128)S(1)}, f32[18,1,128]{2,1,0:T(1,128)S(1)}, u32[]{:S(2)}, u32[]{:S(2)}) collective-permute-start(f32[18,1,128]{2,1,0:T(1,128)S(1)} %get-tuple-element.88), channel_id=1, source_target_pairs={{0,1},{1,2},{2,3},{3,4},{4,5},{5,6},{6,7},{7,8},{8,9},{9,10},{10,1... | collective-permute-start | bytes 27656 | tf_op jit(solution)/shard_map/ppermute | solution.py:24
  224.8 12.1 %collective-permute-start.27 = (f32[18,1,128]{2,1,0:T(1,128)S(1)}, f32[18,1,128]{2,1,0:T(1,128)S(1)}, u32[]{:S(2)}, u32[]{:S(2)}) collective-permute-start(f32[18,1,128]{2,1,0:T(1,128)S(1)} %get-tuple-element.89), channel_id=1, source_target_pairs={{1,0},{2,1},{3,2},{4,3},{5,4},{6,5},{7,6},{8,7},{9,8},{10,9},{11,1... | collective-permute-start | bytes 27656 | tf_op jit(solution)/shard_map/ppermute | solution.py:25
  229.5 18.5 %collective-permute-start.22 = (f32[10,1,64]{2,1,0:T(1,128)}, f32[10,1,64]{2,1,0:T(1,128)}, u32[]{:S(2)}, u32[]{:S(2)}) collective-permute-start(f32[10,1,64]{2,1,0:T(1,128)} %get-tuple-element.115), channel_id=1, source_target_pairs={{0,1},{1,2},{2,3},{3,4},{4,5},{5,6},{6,7},{7,8},{8,9},{9,10},{10,1... | collective-permute-start | bytes 7688 | tf_op jit(solution)/shard_map/ppermute | solution.py:24
  234.8 13.2 %collective-permute-start.23 = (f32[10,1,64]{2,1,0:T(1,128)}, f32[10,1,64]{2,1,0:T(1,128)}, u32[]{:S(2)}, u32[]{:S(2)}) collective-permute-start(f32[10,1,64]{2,1,0:T(1,128)} %get-tuple-element.114), channel_id=1, source_target_pairs={{1,0},{2,1},{3,2},{4,3},{5,4},{6,5},{7,6},{8,7},{9,8},{10,9},{11,1... | collective-permute-start | bytes 7688 | tf_op jit(solution)/shard_map/ppermute | solution.py:25
  249.2 7.1 %collective-permute-start.28 = (f32[1,4,64]{2,1,0:T(4,128)S(1)}, f32[1,4,64]{2,1,0:T(4,128)S(1)}, u32[]{:S(2)}, u32[]{:S(2)}) collective-permute-start(f32[1,4,64]{2,1,0:T(4,128)S(1)} %get-tuple-element.122), channel_id=1, source_target_pairs={{0,32},{32,64},{64,96},{96,128},{128,160},{160,192},{192,224},{1,3... | collective-permute-start | bytes 3080 | tf_op jit(solution)/shard_map/ppermute | solution.py:24
  258.6 68.7 %collective-permute-start.30 = (f32[10,1,64]{2,1,0:T(1,128)S(1)}, f32[10,1,64]{2,1,0:T(1,128)S(1)}, u32[]{:S(2)}, u32[]{:S(2)}) collective-permute-start(f32[10,1,64]{2,1,0:T(1,128)S(1)} %get-tuple-element.112), channel_id=1, source_target_pairs={{0,1},{1,2},{2,3},{3,4},{4,5},{5,6},{6,7},{7,8},{8,9},{9,10},{10,1... | collective-permute-start | bytes 7688 | tf_op jit(solution)/shard_map/ppermute | solution.py:24
  265.6 61.8 %collective-permute-start.31 = (f32[10,1,64]{2,1,0:T(1,128)S(1)}, f32[10,1,64]{2,1,0:T(1,128)S(1)}, u32[]{:S(2)}, u32[]{:S(2)}) collective-permute-start(f32[10,1,64]{2,1,0:T(1,128)S(1)} %get-tuple-element.113), channel_id=1, source_target_pairs={{1,0},{2,1},{3,2},{4,3},{5,4},{6,5},{7,6},{8,7},{9,8},{10,9},{11,1... | collective-permute-start | bytes 7688 | tf_op jit(solution)/shard_map/ppermute | solution.py:25
  328.2 8.2 %collective-permute-start.36 = (f32[1,4,64]{2,1,0:T(4,128)S(1)}, f32[1,4,64]{2,1,0:T(4,128)S(1)}, u32[]{:S(2)}, u32[]{:S(2)}) collective-permute-start(f32[1,4,64]{2,1,0:T(4,128)S(1)} %get-tuple-element.120), channel_id=1, source_target_pairs={{0,32},{32,64},{64,96},{96,128},{128,160},{160,192},{192,224},{1,3... | collective-permute-start | bytes 3080 | tf_op jit(solution)/shard_map/ppermute | solution.py:24
  337.8 13.8 %collective-permute-start.38 = (f32[10,1,64]{2,1,0:T(1,128)S(1)}, f32[10,1,64]{2,1,0:T(1,128)S(1)}, u32[]{:S(2)}, u32[]{:S(2)}) collective-permute-start(f32[10,1,64]{2,1,0:T(1,128)S(1)} %get-tuple-element.110), channel_id=1, source_target_pairs={{0,1},{1,2},{2,3},{3,4},{4,5},{5,6},{6,7},{7,8},{8,9},{9,10},{10,1... | collective-permute-start | bytes 7688 | tf_op jit(solution)/shard_map/ppermute | solution.py:24
  340.5 11.1 %collective-permute-start.39 = (f32[10,1,64]{2,1,0:T(1,128)S(1)}, f32[10,1,64]{2,1,0:T(1,128)S(1)}, u32[]{:S(2)}, u32[]{:S(2)}) collective-permute-start(f32[10,1,64]{2,1,0:T(1,128)S(1)} %get-tuple-element.111), channel_id=1, source_target_pairs={{1,0},{2,1},{3,2},{4,3},{5,4},{6,5},{7,6},{8,7},{9,8},{10,9},{11,1... | collective-permute-start | bytes 7688 | tf_op jit(solution)/shard_map/ppermute | solution.py:25
  343.7 13.3 %collective-permute-start.34 = (f32[6,1,32]{2,0,1:T(8,128)}, f32[6,1,32]{2,0,1:T(8,128)}, u32[]{:S(2)}, u32[]{:S(2)}) collective-permute-start(f32[6,1,32]{2,0,1:T(8,128)} %get-tuple-element.137), channel_id=1, source_target_pairs={{0,1},{1,2},{2,3},{3,4},{4,5},{5,6},{6,7},{7,8},{8,9},{9,10},{10,1... | collective-permute-start | bytes 2312 | tf_op jit(solution)/shard_map/ppermute | solution.py:24
  349.7 8.0 %collective-permute-start.35 = (f32[6,1,32]{2,0,1:T(8,128)}, f32[6,1,32]{2,0,1:T(8,128)}, u32[]{:S(2)}, u32[]{:S(2)}) collective-permute-start(f32[6,1,32]{2,0,1:T(8,128)} %get-tuple-element.136), channel_id=1, source_target_pairs={{1,0},{2,1},{3,2},{4,3},{5,4},{6,5},{7,6},{8,7},{9,8},{10,9},{11,1... | collective-permute-start | bytes 2312 | tf_op jit(solution)/shard_map/ppermute | solution.py:25
  367.6 10.9 %collective-permute-start.42 = (f32[6,1,32]{2,0,1:T(8,128)S(1)}, f32[6,1,32]{2,0,1:T(8,128)S(1)}, u32[]{:S(2)}, u32[]{:S(2)}) collective-permute-start(f32[6,1,32]{2,0,1:T(8,128)S(1)} %get-tuple-element.134), channel_id=1, source_target_pairs={{0,1},{1,2},{2,3},{3,4},{4,5},{5,6},{6,7},{7,8},{8,9},{9,10},{10,1... | collective-permute-start | bytes 2312 | tf_op jit(solution)/shard_map/ppermute | solution.py:24
  372.7 7.7 %collective-permute-start.43 = (f32[6,1,32]{2,0,1:T(8,128)S(1)}, f32[6,1,32]{2,0,1:T(8,128)S(1)}, u32[]{:S(2)}, u32[]{:S(2)}) collective-permute-start(f32[6,1,32]{2,0,1:T(8,128)S(1)} %get-tuple-element.135), channel_id=1, source_target_pairs={{1,0},{2,1},{3,2},{4,3},{5,4},{6,5},{7,6},{8,7},{9,8},{10,9},{11,1... | collective-permute-start | bytes 2312 | tf_op jit(solution)/shard_map/ppermute | solution.py:25
  395.4 8.0 %collective-permute-start.47 = (f32[6,1,32]{2,0,1:T(8,128)}, f32[6,1,32]{2,0,1:T(8,128)}, u32[]{:S(2)}, u32[]{:S(2)}) collective-permute-start(f32[6,1,32]{2,0,1:T(8,128)} %get-tuple-element.133), channel_id=1, source_target_pairs={{1,0},{2,1},{3,2},{4,3},{5,4},{6,5},{7,6},{8,7},{9,8},{10,9},{11,1... | collective-permute-start | bytes 2312 | tf_op jit(solution)/shard_map/ppermute | solution.py:25
  479.7 7.3 %collective-permute-start.48 = (f32[1,2,32]{2,0,1:T(1,128)S(1)}, f32[1,2,32]{2,0,1:T(1,128)S(1)}, u32[]{:S(2)}, u32[]{:S(2)}) collective-permute-start(f32[1,2,32]{2,0,1:T(1,128)S(1)} %get-tuple-element.140), channel_id=1, source_target_pairs={{0,32},{32,64},{64,96},{96,128},{128,160},{160,192},{192,224},{1,3... | collective-permute-start | bytes 776 | tf_op jit(solution)/shard_map/ppermute | solution.py:24
  489.3 7.2 %collective-permute-start.50 = (f32[6,1,32]{2,0,1:T(8,128)S(1)}, f32[6,1,32]{2,0,1:T(8,128)S(1)}, u32[]{:S(2)}, u32[]{:S(2)}) collective-permute-start(f32[6,1,32]{2,0,1:T(8,128)S(1)} %get-tuple-element.130), channel_id=1, source_target_pairs={{0,1},{1,2},{2,3},{3,4},{4,5},{5,6},{6,7},{7,8},{8,9},{9,10},{10,1... | collective-permute-start | bytes 2312 | tf_op jit(solution)/shard_map/ppermute | solution.py:24
  494.5 7.7 %collective-permute-start.51 = (f32[6,1,32]{2,0,1:T(8,128)S(1)}, f32[6,1,32]{2,0,1:T(8,128)S(1)}, u32[]{:S(2)}, u32[]{:S(2)}) collective-permute-start(f32[6,1,32]{2,0,1:T(8,128)S(1)} %get-tuple-element.131), channel_id=1, source_target_pairs={{1,0},{2,1},{3,2},{4,3},{5,4},{6,5},{7,6},{8,7},{9,8},{10,9},{11,1... | collective-permute-start | bytes 2312 | tf_op jit(solution)/shard_map/ppermute | solution.py:25
  513.2 7.7 %collective-permute-start.55 = (f32[6,1,32]{2,0,1:T(8,128)S(1)}, f32[6,1,32]{2,0,1:T(8,128)S(1)}, u32[]{:S(2)}, u32[]{:S(2)}) collective-permute-start(f32[6,1,32]{2,0,1:T(8,128)S(1)} %get-tuple-element.129), channel_id=1, source_target_pairs={{1,0},{2,1},{3,2},{4,3},{5,4},{6,5},{7,6},{8,7},{9,8},{10,9},{11,1... | collective-permute-start | bytes 2312 | tf_op jit(solution)/shard_map/ppermute | solution.py:25
  534.6 7.7 %collective-permute-start.59 = (f32[10,1,64]{2,1,0:T(1,128)S(1)}, f32[10,1,64]{2,1,0:T(1,128)S(1)}, u32[]{:S(2)}, u32[]{:S(2)}) collective-permute-start(f32[10,1,64]{2,1,0:T(1,128)S(1)} %get-tuple-element.109), channel_id=1, source_target_pairs={{1,0},{2,1},{3,2},{4,3},{5,4},{6,5},{7,6},{8,7},{9,8},{10,9},{11,1... | collective-permute-start | bytes 7688 | tf_op jit(solution)/shard_map/ppermute | solution.py:25
  553.2 7.7 %collective-permute-start.63 = (f32[10,1,64]{2,1,0:T(1,128)S(1)}, f32[10,1,64]{2,1,0:T(1,128)S(1)}, u32[]{:S(2)}, u32[]{:S(2)}) collective-permute-start(f32[10,1,64]{2,1,0:T(1,128)S(1)} %get-tuple-element.107), channel_id=1, source_target_pairs={{1,0},{2,1},{3,2},{4,3},{5,4},{6,5},{7,6},{8,7},{9,8},{10,9},{11,1... | collective-permute-start | bytes 7688 | tf_op jit(solution)/shard_map/ppermute | solution.py:25
  579.5 7.7 %collective-permute-start.67 = (f32[18,1,128]{2,1,0:T(1,128)S(1)}, f32[18,1,128]{2,1,0:T(1,128)S(1)}, u32[]{:S(2)}, u32[]{:S(2)}) collective-permute-start(f32[18,1,128]{2,1,0:T(1,128)S(1)} %get-tuple-element.87), channel_id=1, source_target_pairs={{1,0},{2,1},{3,2},{4,3},{5,4},{6,5},{7,6},{8,7},{9,8},{10,9},{11,1... | collective-permute-start | bytes 27656 | tf_op jit(solution)/shard_map/ppermute | solution.py:25
  598.3 7.7 %collective-permute-start.71 = (f32[18,1,128]{2,1,0:T(1,128)S(1)}, f32[18,1,128]{2,1,0:T(1,128)S(1)}, u32[]{:S(2)}, u32[]{:S(2)}) collective-permute-start(f32[18,1,128]{2,1,0:T(1,128)S(1)} %get-tuple-element.85), channel_id=1, source_target_pairs={{1,0},{2,1},{3,2},{4,3},{5,4},{6,5},{7,6},{8,7},{9,8},{10,9},{11,1... | collective-permute-start | bytes 27656 | tf_op jit(solution)/shard_map/ppermute | solution.py:25
  654.5 8.0 %collective-permute-start.75 = (f32[34,1,256]{2,1,0:T(1,128)S(1)}, f32[34,1,256]{2,1,0:T(1,128)S(1)}, u32[]{:S(2)}, u32[]{:S(2)}) collective-permute-start(f32[34,1,256]{2,1,0:T(1,128)S(1)} %get-tuple-element.61), channel_id=1, source_target_pairs={{1,0},{2,1},{3,2},{4,3},{5,4},{6,5},{7,6},{8,7},{9,8},{10,9},{11,1... | collective-permute-start | bytes 104456 | tf_op jit(solution)/shard_map/ppermute | solution.py:25
  673.5 8.0 %collective-permute-start.79 = (f32[34,1,256]{2,1,0:T(1,128)S(1)}, f32[34,1,256]{2,1,0:T(1,128)S(1)}, u32[]{:S(2)}, u32[]{:S(2)}) collective-permute-start(f32[34,1,256]{2,1,0:T(1,128)S(1)} %get-tuple-element.59), channel_id=1, source_target_pairs={{1,0},{2,1},{3,2},{4,3},{5,4},{6,5},{7,6},{8,7},{9,8},{10,9},{11,1... | collective-permute-start | bytes 104456 | tf_op jit(solution)/shard_map/ppermute | solution.py:25
  692.5 8.0 %collective-permute-start.83 = (f32[34,1,256]{2,1,0:T(1,128)S(1)}, f32[34,1,256]{2,1,0:T(1,128)S(1)}, u32[]{:S(2)}, u32[]{:S(2)}) collective-permute-start(f32[34,1,256]{2,1,0:T(1,128)S(1)} %get-tuple-element.57), channel_id=1, source_target_pairs={{1,0},{2,1},{3,2},{4,3},{5,4},{6,5},{7,6},{8,7},{9,8},{10,9},{11,1... | collective-permute-start | bytes 104456 | tf_op jit(solution)/shard_map/ppermute | solution.py:25
  (69 other events, 2280.3 us)
where the time goes:
time: 707 us; the launch traced here: 702 us
  starting transfers between devices  249 us (35%)
  local copies, waits for them, and re-layouts  146 us (21%)
  blocking collectives  117 us (17%)
  waiting for transfers between devices  98.8 us (14%)
  other arithmetic  88.2 us (12%)
    ppermute x42, starting transfers between devices, with_halo(): before = lax.ppermute(last, axis, up)  152 us
    ppermute x42, waiting for transfers between devices, with_halo(): after = lax.ppermute(leading, axis, down)  98.7 us
    ppermute x42, starting transfers between devices, with_halo(): after = lax.ppermute(leading, axis, down)  97.6 us
    reshape x4, local copies, waits for them, and re-layouts, restrict(): field.reshape(size_x // 2, 2, size_y // 2, 2, size_z // 2, 2)  79.5 us
    all_gather x1, blocking collectives, collect(): lax.all_gather(conduct, ('gx', 'gy'), axis=0, tiled=True)  59.7 us
    all_gather x1, blocking collectives, collect(): lax.all_gather(source, ('gx', 'gy'), axis=0, tiled=True)  57.4 us
    reduce_sum x10, other arithmetic, restrict(): jnp.mean(field.reshape(size_x // 2, 2, size_y // 2, 2, size_z // 2, 2), a...  38.5 us
    reshape x3, local copies, waits for them, and re-layouts, prolong(): return grown.reshape(2 * size_x, 2 * size_y, 2 * size_z)  29.9 us
  transfers between devices with their start and end apart: 84, of which 28 were waited for; matrix products, arithmetic and copies ran while one was open for 22% of the time, Pallas kernels for 0%

commit v1 on v0

--- a/solution.py
+++ b/solution.py
@@ -12,6 +12,13 @@
 SMOOTH_HI = 2.0
 COARSE_LO = 0.05
 COARSE_HI = 2.0
+
+
+def all_by_exchange(x, axis, d):
+    size = lax.axis_size(axis)
+    pieces = jnp.stack([x for _ in range(size)])
+    pieces = lax.all_to_all(pieces, axis, split_axis=0, concat_axis=0)
+    return jnp.concatenate(pieces, axis=d)
 
 
 def with_halo(value, sides, width):
@@ -112,7 +119,7 @@
     count_x = lax.axis_size("gx")
     count_y = lax.axis_size("gy")
     gathered = (
-        lax.all_gather(source, ("gx", "gy"), axis=0, tiled=True),
+        all_by_exchange(source, ("gx", "gy"), 0),
         lax.all_gather(conduct, ("gx", "gy"), axis=0, tiled=True),
     )
     arranged = []

time: 707 us -> 677 us (0.958)
  blocking collectives: 117 us -> 63.8 us
  starting transfers between devices: 249 us -> 264 us
  waiting for transfers between devices: 98.8 us -> 107 us
    all_gather x1 -> x0, blocking collectives: 57.4 us -> none  [collect(): lax.all_gather(source, ('gx', 'gy'), axis=0, tiled=True)]
    all_to_all x0 -> x1, starting transfers between devices: none -> 14 us  [all_by_exchange(): pieces = lax.all_to_all(pieces, axis, split_axis=0, concat_axis=0)]
    all_to_all x0 -> x1, waiting for transfers between devices: none -> 7.97 us  [all_by_exchange(): pieces = lax.all_to_all(pieces, axis, split_axis=0, concat_axis=0)]
  transfers between devices with their start and end apart: 84 -> 85, of which waited for: 28 -> 29; matrix products, arithmetic and copies ran while one was open for 22% -> 22% of each run, Pallas kernels for 0% -> 0%
where the time goes in v1:
time: 677 us; the launch traced here: 672 us
  starting transfers between devices  264 us (39%)
  local copies, waits for them, and re-layouts  151 us (22%)
  waiting for transfers between devices  107 us (16%)
  other arithmetic  83.1 us (12%)
  blocking collectives  63.8 us (9%)
    ppermute x42, starting transfers between devices, with_halo(): before = lax.ppermute(last, axis, up)  155 us
    ppermute x42, waiting for transfers between devices, with_halo(): after = lax.ppermute(leading, axis, down)  98.6 us
    ppermute x42, starting transfers between devices, with_halo(): after = lax.ppermute(leading, axis, down)  95.5 us
    reshape x4, local copies, waits for them, and re-layouts, restrict(): field.reshape(size_x // 2, 2, size_y // 2, 2, size_z // 2, 2)  78.9 us
    all_gather x1, blocking collectives, collect(): lax.all_gather(conduct, ('gx', 'gy'), axis=0, tiled=True)  63.8 us
    reduce_sum x10, other arithmetic, restrict(): jnp.mean(field.reshape(size_x // 2, 2, size_y // 2, 2, size_z // 2, 2), a...  37.9 us
    reshape x3, local copies, waits for them, and re-layouts, prolong(): return grown.reshape(2 * size_x, 2 * size_y, 2 * size_z)  29.9 us
    add x14, other arithmetic, chebyshev(): iterate = iterate + update  16.6 us
  transfers between devices with their start and end apart: 85, of which 29 were waited for; matrix products, arithmetic and copies ran while one was open for 22% of the time, Pallas kernels for 0%

profile of v1, /device:TPU:103, one launch (start us, length us, event | category | flops | bytes accessed | tf_op | source)
XLA Modules:
  0.0 671.7 jit_solution(14585589201160788660)
XLA Ops:
  1.4 3.8 collective-permute-start
  8.9 35.7 %reshape.74 = f32[16,2,8,2,128,2]{5,4,3,2,1,0:T(8,128)} reshape(f32[32,16,256]{2,1,0:T(8,128)} %param.3) | data formatting | bytes 1048576 | tf_op jit(solution)/shard_map/reshape | solution.py:100
  44.5 12.2 %reduce_sum.86 = f32[16,8,128]{2,1,0:T(8,128)S(1)} reduce(f32[16,2,8,2,128,2]{5,4,3,2,1,0:T(8,128)} %reshape.74, f32[]{:T(128)} %constant.35.clone.1), dimensions={1,3,5}, to_apply=%region_0.0 | reduce | flops 114688 | bytes 589828 | tf_op jit(solution)/shard_map/reduce_sum | solution.py:100
  56.9 4.7 collective-permute-start.2
  63.5 6.0 collective-permute-done.3
  71.5 5.1 collective-permute-start.4
  78.5 3.6 collective-permute-start.8
  90.2 5.5 div.201
  98.3 3.8 fusion.7
  102.1 4.2 collective-permute-start.12
  111.4 5.0 collective-permute-start.14
  118.4 6.7 collective-permute-start.10
  128.6 35.6 %reshape.75 = f32[16,2,8,2,128,2]{5,4,3,2,1,0:T(8,128)} reshape(f32[32,16,256]{2,1,0:T(8,128)} %fusion.13) | data formatting | bytes 1048576 | tf_op jit(solution)/shard_map/reshape | solution.py:100
  164.1 12.2 %reduce_sum.87 = f32[16,8,128]{2,1,0:T(8,128)S(1)} reduce(f32[16,2,8,2,128,2]{5,4,3,2,1,0:T(8,128)} %reshape.75, f32[]{:T(128)} %constant.35.clone.1), dimensions={1,3,5}, to_apply=%region_1.0 | reduce | flops 114688 | bytes 589828 | tf_op jit(solution)/shard_map/reduce_sum | solution.py:100
  184.8 3.6 collective-permute-start.20
  190.4 7.0 %collective-permute-start.18 = (f32[18,1,128]{2,1,0:T(1,128)S(1)}, f32[18,1,128]{2,1,0:T(1,128)S(1)}, u32[]{:S(2)}, u32[]{:S(2)}) collective-permute-start(f32[18,1,128]{2,1,0:T(1,128)S(1)} %get-tuple-element.88), channel_id=1, source_target_pairs={{0,1},{1,2},{2,3},{3,4},{4,5},{5,6},{6,7},{7,8},{8,9},{9,10},{10,1... | collective-permute-start | bytes 27656 | tf_op jit(solution)/shard_map/ppermute | solution.py:31
  206.6 5.1 collective-permute-start.24
  216.6 4.6 collective-permute-start.26
  224.6 6.7 collective-permute-start.22
  234.5 5.6 reshape.76
  249.3 3.6 collective-permute-start.32
  254.9 7.0 %collective-permute-start.30 = (f32[10,1,64]{2,1,0:T(1,128)S(1)}, f32[10,1,64]{2,1,0:T(1,128)S(1)}, u32[]{:S(2)}, u32[]{:S(2)}) collective-permute-start(f32[10,1,64]{2,1,0:T(1,128)S(1)} %get-tuple-element.110), channel_id=1, source_target_pairs={{0,1},{1,2},{2,3},{3,4},{4,5},{5,6},{6,7},{7,8},{8,9},{9,10},{10,1... | collective-permute-start | bytes 7688 | tf_op jit(solution)/shard_map/ppermute | solution.py:31
  265.2 4.3 collective-permute-done.31
  269.6 5.1 collective-permute-start.36
  285.5 5.2 collective-permute-start.34
  301.5 3.7 collective-permute-start.40
  310.9 4.3 collective-permute-start.42
  317.9 5.3 collective-permute-done.43
  324.8 4.5 collective-permute-start.44
  331.2 63.8 %all-gather.1 = f32[256,2,16]{2,1,0:T(2,128)} all-gather(f32[1,2,16]{2,1,0:T(2,128)S(1)} %multiply_bitcast_fusion), channel_id=2, replica_groups=mesh['gx'=8,'gy'=32] {'gx','gy'}, dimensions={0}, use_global_device_ids=true | all-gather | bytes 32896 | tf_op jit(solution)/shard_map/all_gather | solution.py:123
  396.9 4.4 collective-permute-start.46
  403.8 5.1 collective-permute-done.47
  414.7 14.0 %all-to-all-start = ((f32[256,2,1,16]{3,1,2,0:T(2,128)}), f32[256,2,1,16]{3,1,2,0:T(2,128)}, u32[]{:S(2)}, u32[]{:S(2)}) async-start(f32[256,2,1,16]{3,1,2,0:T(2,128)} %stack.2), calls=%async_computation | async-start | bytes 524288 | tf_op jit(solution)/shard_map/all_to_all | solution.py:20
  430.4 8.0 %all-to-all-done = f32[256,2,1,16]{3,1,2,0:T(2,128)} async-done(((f32[256,2,1,16]{3,1,2,0:T(2,128)}), f32[256,2,1,16]{3,1,2,0:T(2,128)}, u32[]{:S(2)}, u32[]{:S(2)}) %all-to-all-start) | async-done | bytes 32800 | tf_op jit(solution)/shard_map/all_to_all | solution.py:20
  460.4 3.9 collective-permute-start.50
  466.2 5.7 collective-permute-done.51
  486.3 4.3 collective-permute-done.55
  507.7 4.3 collective-permute-done.59
  522.9 3.6 collective-permute-start.63
  526.5 4.1 collective-permute-done.63
  534.1 4.0 reshape.82
  552.4 4.3 collective-permute-done.67
  571.2 4.3 collective-permute-done.71
  576.7 11.4 %broadcast_in_dim.36 = f32[16,2,8,2,128,2]{5,4,3,2,1,0:T(8,128)} broadcast(f32[16,8,128]{2,1,0:T(8,128)S(1)} %fusion.240), dimensions={0,2,4} | broadcast | bytes 589824 | tf_op jit(solution)/shard_map/broadcast_in_dim | solution.py:105
  588.2 24.6 %reshape.83 = f32[32,16,256]{2,1,0:T(8,128)} reshape(f32[16,2,8,2,128,2]{5,4,3,2,1,0:T(8,128)} %broadcast_in_dim.36) | data formatting | bytes 1048576 | tf_op jit(solution)/shard_map/reshape | solution.py:106
  627.6 4.6 collective-permute-done.75
  646.5 4.6 collective-permute-done.79
  665.5 4.6 collective-permute-done.83
  (318 shorter events, 265.9 us)
Async XLA Ops:
  1.4 55.4 %collective-permute-start = (f32[1,16,256]{2,1,0:T(8,128)S(1)}, f32[1,16,256]{2,1,0:T(8,128)S(1)}, u32[]{:S(2)}, u32[]{:S(2)}) collective-permute-start(f32[1,16,256]{2,1,0:T(8,128)S(1)} %get-tuple-element.79), channel_id=1, source_target_pairs={{0,32},{32,64},{64,96},{96,128},{128,160},{160,192},{192,224},{1,3... | collective-permute-start | bytes 49160 | tf_op jit(solution)/shard_map/ppermute | solution.py:31
  5.1 51.7 %collective-permute-start.1 = (f32[1,16,256]{2,1,0:T(8,128)S(1)}, f32[1,16,256]{2,1,0:T(8,128)S(1)}, u32[]{:S(2)}, u32[]{:S(2)}) collective-permute-start(f32[1,16,256]{2,1,0:T(8,128)S(1)} %get-tuple-element.78), channel_id=1, source_target_pairs={{32,0},{64,32},{96,64},{128,96},{160,128},{192,160},{224,192},{33,... | collective-permute-start | bytes 49160 | tf_op jit(solution)/shard_map/ppermute | solution.py:32
  61.6 8.0 %collective-permute-start.3 = (f32[34,1,256]{2,1,0:T(1,128)S(1)}, f32[34,1,256]{2,1,0:T(1,128)S(1)}, u32[]{:S(2)}, u32[]{:S(2)}) collective-permute-start(f32[34,1,256]{2,1,0:T(1,128)S(1)} %get-tuple-element.64), channel_id=1, source_target_pairs={{1,0},{2,1},{3,2},{4,3},{5,4},{6,5},{7,6},{8,7},{9,8},{10,9},{11,1... | collective-permute-start | bytes 104456 | tf_op jit(solution)/shard_map/ppermute | solution.py:32
  71.5 12.6 %collective-permute-start.4 = (f32[1,16,256]{2,1,0:T(8,128)S(1)}, f32[1,16,256]{2,1,0:T(8,128)S(1)}, u32[]{:S(2)}, u32[]{:S(2)}) collective-permute-start(f32[1,16,256]{2,1,0:T(8,128)S(1)} %get-tuple-element.74), channel_id=1, source_target_pairs={{0,32},{32,64},{64,96},{96,128},{128,160},{160,192},{192,224},{1,3... | collective-permute-start | bytes 49160 | tf_op jit(solution)/shard_map/ppermute | solution.py:31
  78.5 39.8 %collective-permute-start.8 = (f32[1,8,128]{2,1,0:T(8,128)S(1)}, f32[1,8,128]{2,1,0:T(8,128)S(1)}, u32[]{:S(2)}, u32[]{:S(2)}) collective-permute-start(f32[1,8,128]{2,1,0:T(8,128)S(1)} %get-tuple-element.102), channel_id=1, source_target_pairs={{0,32},{32,64},{64,96},{96,128},{128,160},{160,192},{192,224},{1,3... | collective-permute-start | bytes 12296 | tf_op jit(solution)/shard_map/ppermute | solution.py:31
  82.1 36.2 %collective-permute-start.9 = (f32[1,8,128]{2,1,0:T(8,128)S(1)}, f32[1,8,128]{2,1,0:T(8,128)S(1)}, u32[]{:S(2)}, u32[]{:S(2)}) collective-permute-start(f32[1,8,128]{2,1,0:T(8,128)S(1)} %get-tuple-element.103), channel_id=1, source_target_pairs={{32,0},{64,32},{96,64},{128,96},{160,128},{192,160},{224,192},{33,... | collective-permute-start | bytes 12296 | tf_op jit(solution)/shard_map/ppermute | solution.py:32
  84.2 14.1 %collective-permute-start.6 = (f32[34,1,256]{2,1,0:T(1,128)S(1)}, f32[34,1,256]{2,1,0:T(1,128)S(1)}, u32[]{:S(2)}, u32[]{:S(2)}) collective-permute-start(f32[34,1,256]{2,1,0:T(1,128)S(1)} %get-tuple-element.62), channel_id=1, source_target_pairs={{0,1},{1,2},{2,3},{3,4},{4,5},{5,6},{6,7},{7,8},{8,9},{9,10},{10,1... | collective-permute-start | bytes 104456 | tf_op jit(solution)/shard_map/ppermute | solution.py:31
  86.1 12.2 %collective-permute-start.7 = (f32[34,1,256]{2,1,0:T(1,128)S(1)}, f32[34,1,256]{2,1,0:T(1,128)S(1)}, u32[]{:S(2)}, u32[]{:S(2)}) collective-permute-start(f32[34,1,256]{2,1,0:T(1,128)S(1)} %get-tuple-element.63), channel_id=1, source_target_pairs={{1,0},{2,1},{3,2},{4,3},{5,4},{6,5},{7,6},{8,7},{9,8},{10,9},{11,1... | collective-permute-start | bytes 104456 | tf_op jit(solution)/shard_map/ppermute | solution.py:32
  111.4 15.6 %collective-permute-start.14 = (f32[34,1,256]{2,1,0:T(1,128)S(1)}, f32[34,1,256]{2,1,0:T(1,128)S(1)}, u32[]{:S(2)}, u32[]{:S(2)}) collective-permute-start(f32[34,1,256]{2,1,0:T(1,128)S(1)} %get-tuple-element.60), channel_id=1, source_target_pairs={{0,1},{1,2},{2,3},{3,4},{4,5},{5,6},{6,7},{7,8},{8,9},{9,10},{10,1... | collective-permute-start | bytes 104456 | tf_op jit(solution)/shard_map/ppermute | solution.py:31
  116.4 10.6 %collective-permute-start.15 = (f32[34,1,256]{2,1,0:T(1,128)S(1)}, f32[34,1,256]{2,1,0:T(1,128)S(1)}, u32[]{:S(2)}, u32[]{:S(2)}) collective-permute-start(f32[34,1,256]{2,1,0:T(1,128)S(1)} %get-tuple-element.61), channel_id=1, source_target_pairs={{1,0},{2,1},{3,2},{4,3},{5,4},{6,5},{7,6},{8,7},{9,8},{10,9},{11,1... | collective-permute-start | bytes 104456 | tf_op jit(solution)/shard_map/ppermute | solution.py:32
  118.4 58.0 %collective-permute-start.10 = (f32[18,1,128]{2,1,0:T(1,128)S(1)}, f32[18,1,128]{2,1,0:T(1,128)S(1)}, u32[]{:S(2)}, u32[]{:S(2)}) collective-permute-start(f32[18,1,128]{2,1,0:T(1,128)S(1)} %get-tuple-element.91), channel_id=1, source_target_pairs={{0,1},{1,2},{2,3},{3,4},{4,5},{5,6},{6,7},{7,8},{8,9},{9,10},{10,1... | collective-permute-start | bytes 27656 | tf_op jit(solution)/shard_map/ppermute | solution.py:31
  125.1 51.3 %collective-permute-start.11 = (f32[18,1,128]{2,1,0:T(1,128)S(1)}, f32[18,1,128]{2,1,0:T(1,128)S(1)}, u32[]{:S(2)}, u32[]{:S(2)}) collective-permute-start(f32[18,1,128]{2,1,0:T(1,128)S(1)} %get-tuple-element.90), channel_id=1, source_target_pairs={{1,0},{2,1},{3,2},{4,3},{5,4},{6,5},{7,6},{8,7},{9,8},{10,9},{11,1... | collective-permute-start | bytes 27656 | tf_op jit(solution)/shard_map/ppermute | solution.py:32
  178.8 11.6 %collective-permute-start.16 = (f32[1,8,128]{2,1,0:T(8,128)S(1)}, f32[1,8,128]{2,1,0:T(8,128)S(1)}, u32[]{:S(2)}, u32[]{:S(2)}) collective-permute-start(f32[1,8,128]{2,1,0:T(8,128)S(1)} %get-tuple-element.98), channel_id=1, source_target_pairs={{0,32},{32,64},{64,96},{96,128},{128,160},{160,192},{192,224},{1,3... | collective-permute-start | bytes 12296 | tf_op jit(solution)/shard_map/ppermute | solution.py:31
  181.6 8.8 %collective-permute-start.17 = (f32[1,8,128]{2,1,0:T(8,128)S(1)}, f32[1,8,128]{2,1,0:T(8,128)S(1)}, u32[]{:S(2)}, u32[]{:S(2)}) collective-permute-start(f32[1,8,128]{2,1,0:T(8,128)S(1)} %get-tuple-element.99), channel_id=1, source_target_pairs={{32,0},{64,32},{96,64},{128,96},{160,128},{192,160},{224,192},{33,... | collective-permute-start | bytes 12296 | tf_op jit(solution)/shard_map/ppermute | solution.py:32
  184.8 38.4 %collective-permute-start.20 = (f32[1,4,64]{2,1,0:T(4,128)}, f32[1,4,64]{2,1,0:T(4,128)S(1)}, u32[]{:S(2)}, u32[]{:S(2)}) collective-permute-start(f32[1,4,64]{2,1,0:T(4,128)} %get-tuple-element.124), channel_id=1, source_target_pairs={{0,32},{32,64},{64,96},{96,128},{128,160},{160,192},{192,224},{1,3... | collective-permute-start | bytes 3080 | tf_op jit(solution)/shard_map/ppermute | solution.py:31
  188.4 34.8 %collective-permute-start.21 = (f32[1,4,64]{2,1,0:T(4,128)}, f32[1,4,64]{2,1,0:T(4,128)}, u32[]{:S(2)}, u32[]{:S(2)}) collective-permute-start(f32[1,4,64]{2,1,0:T(4,128)} %get-tuple-element.125), channel_id=1, source_target_pairs={{32,0},{64,32},{96,64},{128,96},{160,128},{192,160},{224,192},{33,... | collective-permute-start | bytes 3080 | tf_op jit(solution)/shard_map/ppermute | solution.py:32
  190.4 13.6 %collective-permute-start.18 = (f32[18,1,128]{2,1,0:T(1,128)S(1)}, f32[18,1,128]{2,1,0:T(1,128)S(1)}, u32[]{:S(2)}, u32[]{:S(2)}) collective-permute-start(f32[18,1,128]{2,1,0:T(1,128)S(1)} %get-tuple-element.88), channel_id=1, source_target_pairs={{0,1},{1,2},{2,3},{3,4},{4,5},{5,6},{6,7},{7,8},{8,9},{9,10},{10,1... | collective-permute-start | bytes 27656 | tf_op jit(solution)/shard_map/ppermute | solution.py:31
  197.4 7.8 %collective-permute-start.19 = (f32[18,1,128]{2,1,0:T(1,128)S(1)}, f32[18,1,128]{2,1,0:T(1,128)}, u32[]{:S(2)}, u32[]{:S(2)}) collective-permute-start(f32[18,1,128]{2,1,0:T(1,128)S(1)} %get-tuple-element.89), channel_id=1, source_target_pairs={{1,0},{2,1},{3,2},{4,3},{5,4},{6,5},{7,6},{8,7},{9,8},{10,9},{11,1... | collective-permute-start | bytes 27656 | tf_op jit(solution)/shard_map/ppermute | solution.py:32
  206.6 8.2 %collective-permute-start.24 = (f32[1,8,128]{2,1,0:T(8,128)S(1)}, f32[1,8,128]{2,1,0:T(8,128)S(1)}, u32[]{:S(2)}, u32[]{:S(2)}) collective-permute-start(f32[1,8,128]{2,1,0:T(8,128)S(1)} %get-tuple-element.96), channel_id=1, source_target_pairs={{0,32},{32,64},{64,96},{96,128},{128,160},{160,192},{192,224},{1,3... | collective-permute-start | bytes 12296 | tf_op jit(solution)/shard_map/ppermute | solution.py:31
  216.6 16.8 %collective-permute-start.26 = (f32[18,1,128]{2,1,0:T(1,128)S(1)}, f32[18,1,128]{2,1,0:T(1,128)S(1)}, u32[]{:S(2)}, u32[]{:S(2)}) collective-permute-start(f32[18,1,128]{2,1,0:T(1,128)S(1)} %get-tuple-element.86), channel_id=1, source_target_pairs={{0,1},{1,2},{2,3},{3,4},{4,5},{5,6},{6,7},{7,8},{8,9},{9,10},{10,1... | collective-permute-start | bytes 27656 | tf_op jit(solution)/shard_map/ppermute | solution.py:31
  221.3 12.2 %collective-permute-start.27 = (f32[18,1,128]{2,1,0:T(1,128)S(1)}, f32[18,1,128]{2,1,0:T(1,128)S(1)}, u32[]{:S(2)}, u32[]{:S(2)}) collective-permute-start(f32[18,1,128]{2,1,0:T(1,128)S(1)} %get-tuple-element.87), channel_id=1, source_target_pairs={{1,0},{2,1},{3,2},{4,3},{5,4},{6,5},{7,6},{8,7},{9,8},{10,9},{11,1... | collective-permute-start | bytes 27656 | tf_op jit(solution)/shard_map/ppermute | solution.py:32
  224.6 18.0 %collective-permute-start.22 = (f32[10,1,64]{2,1,0:T(1,128)}, f32[10,1,64]{2,1,0:T(1,128)}, u32[]{:S(2)}, u32[]{:S(2)}) collective-permute-start(f32[10,1,64]{2,1,0:T(1,128)} %get-tuple-element.113), channel_id=1, source_target_pairs={{0,1},{1,2},{2,3},{3,4},{4,5},{5,6},{6,7},{7,8},{8,9},{9,10},{10,1... | collective-permute-start | bytes 7688 | tf_op jit(solution)/shard_map/ppermute | solution.py:31
  231.3 11.3 %collective-permute-start.23 = (f32[10,1,64]{2,1,0:T(1,128)}, f32[10,1,64]{2,1,0:T(1,128)}, u32[]{:S(2)}, u32[]{:S(2)}) collective-permute-start(f32[10,1,64]{2,1,0:T(1,128)} %get-tuple-element.112), channel_id=1, source_target_pairs={{1,0},{2,1},{3,2},{4,3},{5,4},{6,5},{7,6},{8,7},{9,8},{10,9},{11,1... | collective-permute-start | bytes 7688 | tf_op jit(solution)/shard_map/ppermute | solution.py:32
  243.8 11.1 %collective-permute-start.28 = (f32[1,4,64]{2,1,0:T(4,128)S(1)}, f32[1,4,64]{2,1,0:T(4,128)S(1)}, u32[]{:S(2)}, u32[]{:S(2)}) collective-permute-start(f32[1,4,64]{2,1,0:T(4,128)S(1)} %get-tuple-element.120), channel_id=1, source_target_pairs={{0,32},{32,64},{64,96},{96,128},{128,160},{160,192},{192,224},{1,3... | collective-permute-start | bytes 3080 | tf_op jit(solution)/shard_map/ppermute | solution.py:31
  246.6 8.3 %collective-permute-start.29 = (f32[1,4,64]{2,1,0:T(4,128)S(1)}, f32[1,4,64]{2,1,0:T(4,128)S(1)}, u32[]{:S(2)}, u32[]{:S(2)}) collective-permute-start(f32[1,4,64]{2,1,0:T(4,128)S(1)} %get-tuple-element.121), channel_id=1, source_target_pairs={{32,0},{64,32},{96,64},{128,96},{160,128},{192,160},{224,192},{33,... | collective-permute-start | bytes 3080 | tf_op jit(solution)/shard_map/ppermute | solution.py:32
  249.3 27.4 %collective-permute-start.32 = (f32[1,2,32]{2,0,1:T(1,128)S(1)}, f32[1,2,32]{2,0,1:T(1,128)S(1)}, u32[]{:S(2)}, u32[]{:S(2)}) collective-permute-start(f32[1,2,32]{2,0,1:T(1,128)S(1)} %get-tuple-element.148), channel_id=1, source_target_pairs={{0,32},{32,64},{64,96},{96,128},{128,160},{160,192},{192,224},{1,3... | collective-permute-start | bytes 776 | tf_op jit(solution)/shard_map/ppermute | solution.py:31
  252.9 23.8 %collective-permute-start.33 = (f32[1,2,32]{2,0,1:T(1,128)S(1)}, f32[1,2,32]{2,0,1:T(1,128)S(1)}, u32[]{:S(2)}, u32[]{:S(2)}) collective-permute-start(f32[1,2,32]{2,0,1:T(1,128)S(1)} %get-tuple-element.149), channel_id=1, source_target_pairs={{32,0},{64,32},{96,64},{128,96},{160,128},{192,160},{224,192},{33,... | collective-permute-start | bytes 776 | tf_op jit(solution)/shard_map/ppermute | solution.py:32
  254.9 10.3 %collective-permute-start.30 = (f32[10,1,64]{2,1,0:T(1,128)S(1)}, f32[10,1,64]{2,1,0:T(1,128)S(1)}, u32[]{:S(2)}, u32[]{:S(2)}) collective-permute-start(f32[10,1,64]{2,1,0:T(1,128)S(1)} %get-tuple-element.110), channel_id=1, source_target_pairs={{0,1},{1,2},{2,3},{3,4},{4,5},{5,6},{6,7},{7,8},{8,9},{9,10},{10,1... | collective-permute-start | bytes 7688 | tf_op jit(solution)/shard_map/ppermute | solution.py:31
  261.8 7.7 %collective-permute-start.31 = (f32[10,1,64]{2,1,0:T(1,128)S(1)}, f32[10,1,64]{2,1,0:T(1,128)S(1)}, u32[]{:S(2)}, u32[]{:S(2)}) collective-permute-start(f32[10,1,64]{2,1,0:T(1,128)S(1)} %get-tuple-element.111), channel_id=1, source_target_pairs={{1,0},{2,1},{3,2},{4,3},{5,4},{6,5},{7,6},{8,7},{9,8},{10,9},{11,1... | collective-permute-start | bytes 7688 | tf_op jit(solution)/shard_map/ppermute | solution.py:32
  269.6 7.7 %collective-permute-start.36 = (f32[1,4,64]{2,1,0:T(4,128)S(1)}, f32[1,4,64]{2,1,0:T(4,128)S(1)}, u32[]{:S(2)}, u32[]{:S(2)}) collective-permute-start(f32[1,4,64]{2,1,0:T(4,128)S(1)} %get-tuple-element.118), channel_id=1, source_target_pairs={{0,32},{32,64},{64,96},{96,128},{128,160},{160,192},{192,224},{1,3... | collective-permute-start | bytes 3080 | tf_op jit(solution)/shard_map/ppermute | solution.py:31
  279.6 13.1 %collective-permute-start.38 = (f32[10,1,64]{2,1,0:T(1,128)S(1)}, f32[10,1,64]{2,1,0:T(1,128)S(1)}, u32[]{:S(2)}, u32[]{:S(2)}) collective-permute-start(f32[10,1,64]{2,1,0:T(1,128)S(1)} %get-tuple-element.108), channel_id=1, source_target_pairs={{0,1},{1,2},{2,3},{3,4},{4,5},{5,6},{6,7},{7,8},{8,9},{9,10},{10,1... | collective-permute-start | bytes 7688 | tf_op jit(solution)/shard_map/ppermute | solution.py:31
  281.6 11.1 %collective-permute-start.39 = (f32[10,1,64]{2,1,0:T(1,128)S(1)}, f32[10,1,64]{2,1,0:T(1,128)S(1)}, u32[]{:S(2)}, u32[]{:S(2)}) collective-permute-start(f32[10,1,64]{2,1,0:T(1,128)S(1)} %get-tuple-element.109), channel_id=1, source_target_pairs={{1,0},{2,1},{3,2},{4,3},{5,4},{6,5},{7,6},{8,7},{9,8},{10,9},{11,1... | collective-permute-start | bytes 7688 | tf_op jit(solution)/shard_map/ppermute | solution.py:32
  285.5 11.7 %collective-permute-start.34 = (f32[6,1,32]{2,0,1:T(8,128)}, f32[6,1,32]{2,0,1:T(8,128)}, u32[]{:S(2)}, u32[]{:S(2)}) collective-permute-start(f32[6,1,32]{2,0,1:T(8,128)} %get-tuple-element.135), channel_id=1, source_target_pairs={{0,1},{1,2},{2,3},{3,4},{4,5},{5,6},{6,7},{7,8},{8,9},{9,10},{10,1... | collective-permute-start | bytes 2312 | tf_op jit(solution)/shard_map/ppermute | solution.py:31
  290.8 8.0 %collective-permute-start.35 = (f32[6,1,32]{2,0,1:T(8,128)}, f32[6,1,32]{2,0,1:T(8,128)}, u32[]{:S(2)}, u32[]{:S(2)}) collective-permute-start(f32[6,1,32]{2,0,1:T(8,128)} %get-tuple-element.134), channel_id=1, source_target_pairs={{1,0},{2,1},{3,2},{4,3},{5,4},{6,5},{7,6},{8,7},{9,8},{10,9},{11,1... | collective-permute-start | bytes 2312 | tf_op jit(solution)/shard_map/ppermute | solution.py:32
  301.5 8.4 %collective-permute-start.40 = (f32[1,2,32]{2,0,1:T(1,128)}, f32[1,2,32]{2,0,1:T(1,128)}, u32[]{:S(2)}, u32[]{:S(2)}) collective-permute-start(f32[1,2,32]{2,0,1:T(1,128)} %get-tuple-element.144), channel_id=1, source_target_pairs={{0,32},{32,64},{64,96},{96,128},{128,160},{160,192},{192,224},{1,3... | collective-permute-start | bytes 776 | tf_op jit(solution)/shard_map/ppermute | solution.py:31
  315.3 7.9 %collective-permute-start.43 = (f32[6,1,32]{2,0,1:T(8,128)S(1)}, f32[6,1,32]{2,0,1:T(8,128)S(1)}, u32[]{:S(2)}, u32[]{:S(2)}) collective-permute-start(f32[6,1,32]{2,0,1:T(8,128)S(1)} %get-tuple-element.133), channel_id=1, source_target_pairs={{1,0},{2,1},{3,2},{4,3},{5,4},{6,5},{7,6},{8,7},{9,8},{10,9},{11,1... | collective-permute-start | bytes 2312 | tf_op jit(solution)/shard_map/ppermute | solution.py:32
  324.8 71.4 %collective-permute-start.44 = (f32[1,2,32]{2,0,1:T(1,128)}, f32[1,2,32]{2,0,1:T(1,128)}, u32[]{:S(2)}, u32[]{:S(2)}) collective-permute-start(f32[1,2,32]{2,0,1:T(1,128)} %get-tuple-element.140), channel_id=1, source_target_pairs={{0,32},{32,64},{64,96},{96,128},{128,160},{160,192},{192,224},{1,3... | collective-permute-start | bytes 776 | tf_op jit(solution)/shard_map/ppermute | solution.py:31
  329.2 66.9 %collective-permute-start.45 = (f32[1,2,32]{2,0,1:T(1,128)}, f32[1,2,32]{2,0,1:T(1,128)}, u32[]{:S(2)}, u32[]{:S(2)}) collective-permute-start(f32[1,2,32]{2,0,1:T(1,128)} %get-tuple-element.141), channel_id=1, source_target_pairs={{32,0},{64,32},{96,64},{128,96},{160,128},{192,160},{224,192},{33,... | collective-permute-start | bytes 776 | tf_op jit(solution)/shard_map/ppermute | solution.py:32
  401.2 7.7 %collective-permute-start.47 = (f32[6,1,32]{2,0,1:T(8,128)S(1)}, f32[6,1,32]{2,0,1:T(8,128)S(1)}, u32[]{:S(2)}, u32[]{:S(2)}) collective-permute-start(f32[6,1,32]{2,0,1:T(8,128)S(1)} %get-tuple-element.131), channel_id=1, source_target_pairs={{1,0},{2,1},{3,2},{4,3},{5,4},{6,5},{7,6},{8,7},{9,8},{10,9},{11,1... | collective-permute-start | bytes 2312 | tf_op jit(solution)/shard_map/ppermute | solution.py:32
  414.7 23.7 %all-to-all-start = ((f32[256,2,1,16]{3,1,2,0:T(2,128)}), f32[256,2,1,16]{3,1,2,0:T(2,128)}, u32[]{:S(2)}, u32[]{:S(2)}) async-start(f32[256,2,1,16]{3,1,2,0:T(2,128)} %stack.2), calls=%async_computation | async-start | bytes 524288 | tf_op jit(solution)/shard_map/all_to_all | solution.py:20
  464.3 7.7 %collective-permute-start.51 = (f32[6,1,32]{2,0,1:T(8,128)S(1)}, f32[6,1,32]{2,0,1:T(8,128)S(1)}, u32[]{:S(2)}, u32[]{:S(2)}) collective-permute-start(f32[6,1,32]{2,0,1:T(8,128)S(1)} %get-tuple-element.129), channel_id=1, source_target_pairs={{1,0},{2,1},{3,2},{4,3},{5,4},{6,5},{7,6},{8,7},{9,8},{10,9},{11,1... | collective-permute-start | bytes 2312 | tf_op jit(solution)/shard_map/ppermute | solution.py:32
  504.3 7.7 %collective-permute-start.59 = (f32[10,1,64]{2,1,0:T(1,128)S(1)}, f32[10,1,64]{2,1,0:T(1,128)S(1)}, u32[]{:S(2)}, u32[]{:S(2)}) collective-permute-start(f32[10,1,64]{2,1,0:T(1,128)S(1)} %get-tuple-element.107), channel_id=1, source_target_pairs={{1,0},{2,1},{3,2},{4,3},{5,4},{6,5},{7,6},{8,7},{9,8},{10,9},{11,1... | collective-permute-start | bytes 7688 | tf_op jit(solution)/shard_map/ppermute | solution.py:32
  522.9 7.7 %collective-permute-start.63 = (f32[10,1,64]{2,1,0:T(1,128)S(1)}, f32[10,1,64]{2,1,0:T(1,128)S(1)}, u32[]{:S(2)}, u32[]{:S(2)}) collective-permute-start(f32[10,1,64]{2,1,0:T(1,128)S(1)} %get-tuple-element.105), channel_id=1, source_target_pairs={{1,0},{2,1},{3,2},{4,3},{5,4},{6,5},{7,6},{8,7},{9,8},{10,9},{11,1... | collective-permute-start | bytes 7688 | tf_op jit(solution)/shard_map/ppermute | solution.py:32
  549.0 7.7 %collective-permute-start.67 = (f32[18,1,128]{2,1,0:T(1,128)S(1)}, f32[18,1,128]{2,1,0:T(1,128)S(1)}, u32[]{:S(2)}, u32[]{:S(2)}) collective-permute-start(f32[18,1,128]{2,1,0:T(1,128)S(1)} %get-tuple-element.85), channel_id=1, source_target_pairs={{1,0},{2,1},{3,2},{4,3},{5,4},{6,5},{7,6},{8,7},{9,8},{10,9},{11,1... | collective-permute-start | bytes 27656 | tf_op jit(solution)/shard_map/ppermute | solution.py:32
  567.9 7.7 %collective-permute-start.71 = (f32[18,1,128]{2,1,0:T(1,128)S(1)}, f32[18,1,128]{2,1,0:T(1,128)S(1)}, u32[]{:S(2)}, u32[]{:S(2)}) collective-permute-start(f32[18,1,128]{2,1,0:T(1,128)S(1)} %get-tuple-element.83), channel_id=1, source_target_pairs={{1,0},{2,1},{3,2},{4,3},{5,4},{6,5},{7,6},{8,7},{9,8},{10,9},{11,1... | collective-permute-start | bytes 27656 | tf_op jit(solution)/shard_map/ppermute | solution.py:32
  624.2 8.0 %collective-permute-start.75 = (f32[34,1,256]{2,1,0:T(1,128)S(1)}, f32[34,1,256]{2,1,0:T(1,128)S(1)}, u32[]{:S(2)}, u32[]{:S(2)}) collective-permute-start(f32[34,1,256]{2,1,0:T(1,128)S(1)} %get-tuple-element.59), channel_id=1, source_target_pairs={{1,0},{2,1},{3,2},{4,3},{5,4},{6,5},{7,6},{8,7},{9,8},{10,9},{11,1... | collective-permute-start | bytes 104456 | tf_op jit(solution)/shard_map/ppermute | solution.py:32
  643.1 8.0 %collective-permute-start.79 = (f32[34,1,256]{2,1,0:T(1,128)S(1)}, f32[34,1,256]{2,1,0:T(1,128)S(1)}, u32[]{:S(2)}, u32[]{:S(2)}) collective-permute-start(f32[34,1,256]{2,1,0:T(1,128)S(1)} %get-tuple-element.57), channel_id=1, source_target_pairs={{1,0},{2,1},{3,2},{4,3},{5,4},{6,5},{7,6},{8,7},{9,8},{10,9},{11,1... | collective-permute-start | bytes 104456 | tf_op jit(solution)/shard_map/ppermute | solution.py:32
  662.1 8.0 %collective-permute-start.83 = (f32[34,1,256]{2,1,0:T(1,128)S(1)}, f32[34,1,256]{2,1,0:T(1,128)S(1)}, u32[]{:S(2)}, u32[]{:S(2)}) collective-permute-start(f32[34,1,256]{2,1,0:T(1,128)S(1)} %get-tuple-element.55), channel_id=1, source_target_pairs={{1,0},{2,1},{3,2},{4,3},{5,4},{6,5},{7,6},{8,7},{9,8},{10,9},{11,1... | collective-permute-start | bytes 104456 | tf_op jit(solution)/shard_map/ppermute | solution.py:32
  (71 other events, 2896.8 us)
